TPU v7x, 32 devices: a whole 2x2x4 slice. The times are simulated.
32 devices in a mesh: fsdp: 4 (over y, x), context: 4 (over z), tensor: 2 (over core).
Axes of the slice: x: 2, y: 2, z: 4, core: 2. Of those that a mesh axis runs over, the one named last changes fastest.
Arguments:
- tokens: bfloat16 [12288, 768], P(('fsdp', 'context')), may hold values from -6 to 6
- cotangent: bfloat16 [12288, 768], P(('fsdp', 'context')), may hold values from -6 to 6
- w_qkv: bfloat16 [3, 768, 768], P(None, 'fsdp', 'tensor'), may hold values from -0.21875 to 0.21875
- bias_qv: float32 [2, 768], P(None, 'tensor'), may hold values from -3 to 3
- w_attn_out: bfloat16 [768, 768], P('tensor', 'fsdp'), may hold values from -1.25 to 1.25
- w_up: bfloat16 [768, 3072], P('fsdp', 'tensor'), may hold values from -0.21875 to 0.21875
- bias_up: float32 [3072], P('tensor'), may hold values from -3 to 3
- w_down: bfloat16 [3072, 768], P('tensor', 'fsdp'), may hold values from -0.109375 to 0.109375
- gains: float32 [2, 768], replicated, may hold values from 0.1 to 1.9
- shifts: float32 [4, 768], replicated, may hold values from -3 to 3
- seq_lengths: int32 [4, 3], P('fsdp'), may hold values from 1 to 1536, 3072 in all within a row
- key_mask: int32 [12288], P('fsdp'), may hold values 0 or 1
Outputs:
- out: bfloat16 [12288, 768], P(('fsdp', 'context'))
- grad_tokens: bfloat16 [12288, 768], P(('fsdp', 'context'))
- grad_qkv: float32 [3, 768, 768], P(None, 'fsdp', 'tensor')
- grad_attn_out: float32 [768, 768], P('tensor', 'fsdp')
- grad_up: float32 [768, 3072], P('fsdp', 'tensor')
- grad_down: float32 [3072, 768], P('tensor', 'fsdp')
- grad_bias_qv: float32 [2, 768], P(None, 'tensor')
- grad_bias_up: float32 [3072], P('tensor')
- grad_gains: float32 [2, 768], replicated
- grad_shifts: float32 [4, 768], replicated
Inputs may be any that keep to these rules, and one draw needn't show every extreme that they name: `seq_lengths`: row f holds the lengths of the 3 sequences packed in order into the 3072 rows of group f; they sum to 3072 and the longest is 1536 in every row. `key_mask`: 1 marks a row that other rows of its sequence attend to; every row attends to itself.
All inputs are finite; a program needn't handle non-finite values. No bound on the sum of `key_mask` on one device may be relied on, other than what follows from the above.
Results may differ from a plain program's by a relative error of at most 0.022.
Values may be sent and summed in bfloat16 or wider, within the bound.
No kernel may reach another device: no remote copies, remote signals or barrier semaphores. Data moves between devices by JAX's collectives and lax.ppermute only.
A program may use at most 192 MiB of HBM per device.

v0:
```python
import jax
import jax.numpy as jnp
from jax import lax
from jax.sharding import PartitionSpec as P

EPSILON = 1e-12
SCORE_SCALE = 0.125
MASKED_SCORE = -1e30


def normalize(inputs):
    center = inputs - jnp.mean(inputs, axis=-1, keepdims=True)
    factor = lax.rsqrt(jnp.mean(center * center, axis=-1, keepdims=True) + EPSILON)
    return (center * factor, factor)


def norm_back(upstream, normed, factor, gain):
    scaled = upstream * gain
    return factor * (
        scaled
        - jnp.mean(scaled, axis=-1, keepdims=True)
        - normed * jnp.mean(scaled * normed, axis=-1, keepdims=True)
    )


def segment_ids(lengths_row, places):
    bounds = jnp.cumsum(lengths_row)
    return jnp.sum((places[:, None] >= bounds[None, :-1]).astype(jnp.int32), axis=1)


def split_heads(matrix, heads_here):
    return matrix.reshape(matrix.shape[0], heads_here, 64).transpose(1, 0, 2)


def join_heads(stacked):
    return stacked.transpose(1, 0, 2).reshape(stacked.shape[1], stacked.shape[0] * stacked.shape[2])


def score_grads(query_head, key_head, value_head, grad_head, log_head, delta_head, allowed):
    scores = (
        jnp.einsum("qd,kd->qk", query_head, key_head, preferred_element_type=jnp.float32)
        * SCORE_SCALE
    )
    probs = jnp.where(allowed, jnp.exp(scores - log_head[:, None]), 0.0)
    grad_prob = jnp.einsum("qd,kd->qk", grad_head, value_head, preferred_element_type=jnp.float32)
    grad_score = (probs * (grad_prob - delta_head[:, None])).astype(jnp.bfloat16)
    return (probs, grad_score)


def shards(
    tokens,
    cotangent,
    w_qkv,
    bias_qv,
    w_attn_out,
    w_up,
    bias_up,
    w_down,
    gains,
    shifts,
    seq_lengths,
    key_mask,
):
    row_count = tokens.shape[0]
    local_width = w_qkv.shape[2]
    heads_here = local_width // 64
    query_places = lax.axis_index("context") * row_count + jnp.arange(row_count, dtype=jnp.int32)
    lengths_row = seq_lengths[0]
    query_segment = segment_ids(lengths_row, query_places)

    def visible(length):
        key_places = jnp.arange(length, dtype=jnp.int32)
        key_segment = segment_ids(lengths_row, key_places)
        same = query_segment[:, None] == key_segment[None, :]
        return same & ((key_mask[None, :] == 1) | (query_places[:, None] == key_places[None, :]))

    w_proj, w_back, w_upper, w_lower = (
        lax.all_gather(w_qkv, "fsdp", axis=1, tiled=True),
        lax.all_gather(w_attn_out, "fsdp", axis=1, tiled=True),
        lax.all_gather(w_up, "fsdp", axis=0, tiled=True),
        lax.all_gather(w_down, "fsdp", axis=1, tiled=True),
    )
    projected = jnp.einsum("td,kde->kte", tokens, w_proj, preferred_element_type=jnp.float32)
    query = (projected[0] + bias_qv[0]).astype(jnp.bfloat16)
    key_rows = projected[1].astype(jnp.bfloat16)
    value_rows = (projected[2] + bias_qv[1]).astype(jnp.bfloat16)
    query_heads = split_heads(query, heads_here)
    start_state = (
        jnp.full((heads_here, row_count), MASKED_SCORE, jnp.float32),
        jnp.zeros((heads_here, row_count), jnp.float32),
        jnp.zeros((heads_here, row_count, 64), jnp.float32),
    )
    key_piece = lax.all_gather(key_rows, "context", axis=0, tiled=True)
    value_piece = lax.all_gather(value_rows, "context", axis=0, tiled=True)
    allowed = visible(key_piece.shape[0])

    def one_head(inputs):
        query_head, key_head, value_head, running_peak, running_total, running_sum = inputs
        scores = (
            jnp.einsum("qd,kd->qk", query_head, key_head, preferred_element_type=jnp.float32)
            * SCORE_SCALE
        )
        new_peak = jnp.maximum(
            running_peak, jnp.max(jnp.where(allowed, scores, MASKED_SCORE), axis=1)
        )
        weights = jnp.where(allowed, jnp.exp(scores - new_peak[:, None]), 0.0)
        fade = jnp.exp(running_peak - new_peak)
        new_total = running_total * fade + jnp.sum(weights, axis=1)
        new_sum = running_sum * fade[:, None] + jnp.dot(
            weights.astype(jnp.bfloat16), value_head, preferred_element_type=jnp.float32
        )
        return (new_peak, new_total, new_sum)

    peak, total, summed = lax.map(
        one_head,
        (
            query_heads,
            split_heads(key_piece, heads_here),
            split_heads(value_piece, heads_here),
            start_state[0],
            start_state[1],
            start_state[2],
        ),
    )
    attended = join_heads(summed / total[:, :, None]).astype(jnp.bfloat16)
    log_total = peak + jnp.log(total)
    branch_part = jnp.dot(attended, w_back, preferred_element_type=jnp.float32)
    first_sum = (
        tokens.astype(jnp.float32)
        + lax.psum(branch_part.astype(jnp.bfloat16), "tensor").astype(jnp.float32)
        + shifts[0]
    )
    normed1, factor1 = normalize(first_sum)
    first = normed1 * gains[0] + shifts[1]
    first_low = first.astype(jnp.bfloat16)
    upper = jnp.dot(first_low, w_upper, preferred_element_type=jnp.float32) + bias_up
    active_f, gelu_back = jax.vjp(lambda values: jax.nn.gelu(values, approximate=False), upper)
    active = active_f.astype(jnp.bfloat16)
    lower_part = jnp.dot(active, w_lower, preferred_element_type=jnp.float32)
    second_sum = (
        first + lax.psum(lower_part.astype(jnp.bfloat16), "tensor").astype(jnp.float32) + shifts[2]
    )
    normed2, factor2 = normalize(second_sum)
    out = (normed2 * gains[1] + shifts[3]).astype(jnp.bfloat16)
    upstream = cotangent.astype(jnp.float32)
    gain_two = jnp.sum(upstream * normed2, axis=0)
    shift_three = jnp.sum(upstream, axis=0)
    grad_second = norm_back(upstream, normed2, factor2, gains[1])
    shift_two = jnp.sum(grad_second, axis=0)
    lower_grad = grad_second.astype(jnp.bfloat16)
    grad_lower = jnp.einsum("tf,td->fd", active, lower_grad, preferred_element_type=jnp.float32)
    grad_active = jnp.einsum("td,fd->tf", lower_grad, w_lower, preferred_element_type=jnp.float32)
    grad_upper = gelu_back(grad_active)[0].astype(jnp.bfloat16)
    grad_bias_up = jnp.sum(grad_upper.astype(jnp.float32), axis=0)
    grad_upper_w = jnp.einsum(
        "td,tf->df", first_low, grad_upper, preferred_element_type=jnp.float32
    )
    back_part = jnp.einsum("tf,df->td", grad_upper, w_upper, preferred_element_type=jnp.float32)
    grad_first = grad_second + lax.psum(back_part.astype(jnp.bfloat16), "tensor").astype(
        jnp.float32
    )
    gain_one = jnp.sum(grad_first * normed1, axis=0)
    shift_one = jnp.sum(grad_first, axis=0)
    grad_first_sum = norm_back(grad_first, normed1, factor1, gains[0])
    shift_zero = jnp.sum(grad_first_sum, axis=0)
    branch_grad = grad_first_sum.astype(jnp.bfloat16)
    grad_back_w = jnp.einsum("te,td->ed", attended, branch_grad, preferred_element_type=jnp.float32)
    grad_attended = jnp.einsum(
        "td,ed->te", branch_grad, w_back, preferred_element_type=jnp.float32
    ).astype(jnp.bfloat16)
    grad_heads = split_heads(grad_attended, heads_here)
    delta = jnp.sum(
        grad_heads.astype(jnp.float32) * split_heads(attended, heads_here).astype(jnp.float32),
        axis=-1,
    )
    grad_query = jnp.zeros((heads_here, row_count, 64), jnp.float32)
    key_piece = lax.all_gather(key_rows, "context", axis=0, tiled=True)
    value_piece = lax.all_gather(value_rows, "context", axis=0, tiled=True)
    length = key_piece.shape[0]
    attend_allowed = visible(length)

    def one_head(inputs):
        query_head, key_head, value_head, grad_head, log_head, delta_head, grad_query_head = inputs
        probs, grad_score = score_grads(
            query_head, key_head, value_head, grad_head, log_head, delta_head, attend_allowed
        )
        grad_value = jnp.einsum(
            "qk,qd->kd", probs.astype(jnp.bfloat16), grad_head, preferred_element_type=jnp.float32
        )
        grad_query_head = (
            grad_query_head
            + jnp.einsum("qk,kd->qd", grad_score, key_head, preferred_element_type=jnp.float32)
            * SCORE_SCALE
        )
        grad_key = (
            jnp.einsum("qk,qd->kd", grad_score, query_head, preferred_element_type=jnp.float32)
            * SCORE_SCALE
        )
        return (grad_query_head, grad_key, grad_value)

    grad_query, key_terms, value_terms = lax.map(
        one_head,
        (
            query_heads,
            split_heads(key_piece, heads_here),
            split_heads(value_piece, heads_here),
            grad_heads,
            log_total,
            delta,
            grad_query,
        ),
    )
    grad_keys = join_heads(key_terms)
    grad_values = join_heads(value_terms)
    grad_keys_here, grad_values_here = (
        lax.psum_scatter(
            grad_keys.astype(jnp.bfloat16), "context", scatter_dimension=0, tiled=True
        ).astype(jnp.float32),
        lax.psum_scatter(
            grad_values.astype(jnp.bfloat16), "context", scatter_dimension=0, tiled=True
        ).astype(jnp.float32),
    )
    grad_query_low = join_heads(grad_query).astype(jnp.bfloat16)
    stacked = jnp.stack(
        [grad_query_low, grad_keys_here.astype(jnp.bfloat16), grad_values_here.astype(jnp.bfloat16)]
    )
    grad_proj = jnp.einsum("td,kte->kde", tokens, stacked, preferred_element_type=jnp.float32)
    grad_bias_qv = jnp.stack(
        [
            jnp.sum(stacked[0].astype(jnp.float32), axis=0),
            jnp.sum(stacked[2].astype(jnp.float32), axis=0),
        ]
    )
    input_part = jnp.einsum("kte,kde->td", stacked, w_proj, preferred_element_type=jnp.float32)
    grad_tokens = (
        grad_first_sum + lax.psum(input_part.astype(jnp.bfloat16), "tensor").astype(jnp.float32)
    ).astype(jnp.bfloat16)
    part_qkv, part_back, part_upper, part_lower = (
        lax.psum_scatter(
            grad_proj.astype(jnp.bfloat16), "fsdp", scatter_dimension=1, tiled=True
        ).astype(jnp.float32),
        lax.psum_scatter(
            grad_back_w.astype(jnp.bfloat16), "fsdp", scatter_dimension=1, tiled=True
        ).astype(jnp.float32),
        lax.psum_scatter(
            grad_upper_w.astype(jnp.bfloat16), "fsdp", scatter_dimension=0, tiled=True
        ).astype(jnp.float32),
        lax.psum_scatter(
            grad_lower.astype(jnp.bfloat16), "fsdp", scatter_dimension=1, tiled=True
        ).astype(jnp.float32),
    )
    share_qkv, share_back, share_upper, share_lower = (
        lax.psum(part_qkv.astype(jnp.bfloat16), "context").astype(jnp.float32),
        lax.psum(part_back.astype(jnp.bfloat16), "context").astype(jnp.float32),
        lax.psum(part_upper.astype(jnp.bfloat16), "context").astype(jnp.float32),
        lax.psum(part_lower.astype(jnp.bfloat16), "context").astype(jnp.float32),
    )
    gain_rows = jnp.stack([gain_one, gain_two])
    shift_rows = jnp.stack([shift_zero, shift_one, shift_two, shift_three])
    sum_bias_qv, sum_bias_up, sum_gains, sum_shifts = lax.psum(
        (grad_bias_qv, grad_bias_up, gain_rows, shift_rows), ("fsdp", "context")
    )
    return (
        out,
        grad_tokens,
        share_qkv,
        share_back,
        share_upper,
        share_lower,
        sum_bias_qv,
        sum_bias_up,
        sum_gains,
        sum_shifts,
    )


def solution(mesh):
    return jax.shard_map(
        shards,
        mesh=mesh,
        in_specs=(
            P(("fsdp", "context"), None),
            P(("fsdp", "context"), None),
            P(None, "fsdp", "tensor"),
            P(None, "tensor"),
            P("tensor", "fsdp"),
            P("fsdp", "tensor"),
            P("tensor"),
            P("tensor", "fsdp"),
            P(),
            P(),
            P("fsdp", None),
            P("fsdp"),
        ),
        out_specs=(
            P(("fsdp", "context"), None),
            P(("fsdp", "context"), None),
            P(None, "fsdp", "tensor"),
            P("tensor", "fsdp"),
            P("fsdp", "tensor"),
            P("tensor", "fsdp"),
            P(None, "tensor"),
            P("tensor"),
            P(),
            P(),
        ),
        check_vma=False,
    )
```

profile of v0, /device:TPU:0, one launch (start us, length us, event | category | flops | bytes accessed | tf_op | source)
XLA Modules:
  0.0 912.2 jit_solution(13213322940845944234)
XLA Ops:
  8.0 37.1 %all-gather.7.cloned.1.call-done = bf16[3,768,384]{2,1,0:T(8,128)(2,1)} async-done(((bf16[3,192,384]{2,1,0:T(8,128)(2,1)}), bf16[3,768,384]{2,1,0:T(8,128)(2,1)}) %all-gather.7.cloned.1.call-update) | async-done | bytes 1769488 | tf_op jit(solution)/shard_map/all_gather | solution.py:78
  45.1 3.4 convolution_bitcast_fusion
  54.5 10.9 %all_gather.23 = bf16[384,768]{0,1:T(8,128)(2,1)} all-gather(bf16[384,192]{0,1:T(8,128)(2,1)S(1)} %copy-done.28), channel_id=1, replica_groups=mesh['fsdp'=4,'context'=4,'tensor'=2] {'fsdp'}, dimensions={1}, use_global_device_ids=true | all-gather | bytes 737280 | tf_op jit(solution)/shard_map/all_gather | solution.py:79
  69.7 31.6 %all-gather.15.cloned.1.call-done = bf16[1,3072,384]{1,2,0:T(8,128)(2,1)} async-done(((bf16[1,768,384]{1,2,0:T(8,128)(2,1)}), bf16[1,3072,384]{1,2,0:T(8,128)(2,1)}) %all-gather.15.cloned.1.call-update) | async-done | bytes 2359312 | tf_op jit(solution)/shard_map/all_gather | solution.py:93
  101.3 5.7 copy.51
  107.0 45.2 %all-gather.9.cloned.1.call-done = bf16[3072,384]{0,1:T(8,128)(2,1)} async-done(((bf16[768,384]{0,1:T(8,128)(2,1)}), bf16[3072,384]{0,1:T(8,128)(2,1)}) %all-gather.9.cloned.1.call-update) | async-done | bytes 2359312 | tf_op jit(solution)/shard_map/all_gather | solution.py:94
  152.2 5.8 copy.52
  158.0 92.7 %while.32 = (s32[]{:T(128)}, f32[6,768]{1,0:T(8,128)S(1)}, f32[6,768]{1,0:T(8,128)S(1)}, f32[6,768,64]{1,2,0:T(8,128)S(1)}, bf16[6,768,64]{2,1,0:T(8,128)(2,1)},...) while((s32[]{:T(128)}, f32[6,768]{1,0:T(8,128)S(1)}, ...), condition=%wide.region_6.7_spmd.clone.clone, body=%wide.region_3.6_spmd.clone.sunk.clone | while | flops 658295808 | bytes 30400636 | solution.py:114
  158.1 5.0 select_reduce_fusion.3
  163.1 4.8 fusion.154
  167.9 5.4 fusion.155
  173.5 5.0 select_reduce_fusion.3
  178.5 4.8 fusion.154
  183.4 5.4 fusion.155
  189.0 5.0 select_reduce_fusion.3
  194.0 4.8 fusion.154
  198.8 5.4 fusion.155
  204.4 5.0 select_reduce_fusion.3
  209.4 4.8 fusion.154
  214.2 5.4 fusion.155
  219.8 5.0 select_reduce_fusion.3
  224.8 4.8 fusion.154
  229.7 5.4 fusion.155
  235.3 5.0 select_reduce_fusion.3
  240.3 4.8 fusion.154
  245.1 5.4 fusion.155
  256.0 17.0 %all-reduce.8.cloned.1.call-done = bf16[768,768]{1,0:T(8,128)(2,1)} async-done(((bf16[768,768]{1,0:T(8,128)(2,1)}), bf16[768,768]{1,0:T(8,128)(2,1)}) %all-reduce.8.cloned.1.call-update) | async-done | bytes 1179664 | tf_op jit(solution)/shard_map/psum | solution.py:130
  275.5 37.7 %all-gather.11.cloned.1.call-done = bf16[768,1536]{1,0:T(8,128)(2,1)} async-done(((bf16[192,1536]{1,0:T(8,128)(2,1)}), bf16[768,1536]{1,0:T(8,128)(2,1)}) %all-gather.11.cloned.1.call-update) | async-done | bytes 2359312 | tf_op jit(solution)/shard_map/all_gather | solution.py:80
  313.3 15.5 %multiply_convert_fusion.1 = (bf16[768,1536]{1,0:T(8,128)(2,1)}, f32[768,1536]{1,0:T(8,128)}, f32[768,1536]{1,0:T(8,128)}) fusion(f32[1536]{0:T(1024)S(1)} %copy-done.48, bf16[768,1536]{1,0:T(8,128)(2,1)} %all-gather.11.cloned.1.call-done, f32[768]{0:T(1024)S(1)} %get-tuple-element.273, f32[768]{0:T(1024)S(1)} %get-tuple-element.277, ...), kind=kOutput, calls=%fused_computation.67 | convolution fusion | flops 1895104512 | bytes 16536576 | tf_op jit(solution)/shard_map/dot_general | solution.py:136
  328.7 23.6 %all-gather.13.cloned.1.call-done = bf16[1536,768]{0,1:T(8,128)(2,1)} async-done(((bf16[1536,192]{0,1:T(8,128)(2,1)}), bf16[1536,768]{0,1:T(8,128)(2,1)}) %all-gather.13.cloned.1.call-update) | async-done | bytes 2359312 | tf_op jit(solution)/shard_map/all_gather | solution.py:81
  352.3 5.4 convolution_convert_fusion.4
  357.8 19.8 %all-reduce.10.cloned.1.call-done = bf16[768,768]{1,0:T(8,128)(2,1)} async-done(((bf16[768,768]{1,0:T(8,128)(2,1)}), bf16[768,768]{1,0:T(8,128)(2,1)}) %all-reduce.10.cloned.1.call-update) | async-done | bytes 1179664 | tf_op jit(solution)/shard_map/psum | solution.py:141
  384.8 7.2 convert_reduce_fusion
  398.5 19.1 %all-reduce.12.cloned.1.call-done = bf16[768,768]{1,0:T(8,128)(2,1)} async-done(((bf16[768,768]{1,0:T(8,128)(2,1)}), bf16[768,768]{1,0:T(8,128)(2,1)}) %all-reduce.12.cloned.1.call-update) | async-done | bytes 1179664 | tf_op jit(solution)/shard_map/psum | solution.py:159
  417.6 3.9 multiply_reduce_fusion
  426.4 106.2 %while.33 = (s32[]{:T(128)}, bf16[6,768,64]{1,2,0:T(8,128)(2,1)}, bf16[6,3072,64]{1,2,0:T(8,128)(2,1)}, bf16[6,3072,64]{1,2,0:T(8,128)(2,1)}, bf16[6,768,64]{2,1...) while((s32[]{:T(128)}, bf16[6,768,64]{1,2,0:T(8,128)(2,1)}, ...), condition=%wide.region_20.21_spmd.clone.clone, body=%wide.region_19.20_spmd.clone.sunk.clone | while | flops 1536147456 | bytes 51950792 | solution.py:201
  427.2 5.4 exponential_select_fusion.4
  435.2 3.3 multiply_convert_fusion.4
  444.9 5.4 exponential_select_fusion.4
  452.9 3.3 multiply_convert_fusion.4
  462.6 5.4 exponential_select_fusion.4
  470.6 3.3 multiply_convert_fusion.4
  480.3 5.4 exponential_select_fusion.4
  488.3 3.3 multiply_convert_fusion.4
  498.0 5.4 exponential_select_fusion.4
  506.0 3.3 multiply_convert_fusion.4
  515.7 5.4 exponential_select_fusion.4
  523.7 3.3 multiply_convert_fusion.4
  532.6 4.3 copy.54
  537.0 4.3 copy.55
  543.6 42.3 %reduce-scatter.9.cloned.1.call-done = bf16[768,384]{1,0:T(8,128)(2,1)} async-done(((bf16[3072,384]{1,0:T(8,128)(2,1)}), bf16[768,384]{1,0:T(8,128)(2,1)}) %reduce-scatter.9.cloned.1.call-update) | async-done | bytes 589840 | tf_op jit(solution)/shard_map/reduce_scatter | solution.py:216
  586.0 49.3 %reduce-scatter.11.cloned.1.call-done = bf16[768,384]{1,0:T(8,128)(2,1)} async-done(((bf16[3072,384]{1,0:T(8,128)(2,1)}), bf16[768,384]{1,0:T(8,128)(2,1)}) %reduce-scatter.11.cloned.1.call-update) | async-done | bytes 589840 | tf_op jit(solution)/shard_map/reduce_scatter | solution.py:219
  635.3 4.2 convert_bitcast_fusion
  639.5 5.2 copy.60
  644.7 3.2 copy.63
  650.7 5.9 convolution_convert_fusion
  657.4 5.9 convolution_convert_fusion.1
  664.5 4.4 bitcast_convert_fusion
  669.1 10.8 %reduce-scatter.19.cloned.1.call-done = bf16[192,1152]{1,0:T(8,128)(2,1)} async-done(((bf16[768,1152]{1,0:T(8,128)(2,1)}), bf16[192,1152]{1,0:T(8,128)(2,1)}) %reduce-scatter.19.cloned.1.call-update) | async-done | bytes 442384
  682.6 26.1 %reduce-scatter.13.cloned.1.call-done = bf16[384,192]{0,1:T(8,128)(2,1)} async-done(((bf16[384,768]{0,1:T(8,128)(2,1)}), bf16[384,192]{0,1:T(8,128)(2,1)}) %reduce-scatter.13.cloned.1.call-update) | async-done | bytes 147472 | tf_op jit(solution)/shard_map/reduce_scatter | solution.py:242
  708.7 40.4 %reduce-scatter.17.cloned.1.call-done = bf16[1536,192]{0,1:T(8,128)(2,1)} async-done(((bf16[1536,768]{0,1:T(8,128)(2,1)}), bf16[1536,192]{0,1:T(8,128)(2,1)}) %reduce-scatter.17.cloned.1.call-update) | async-done | bytes 589840 | tf_op jit(solution)/shard_map/reduce_scatter | solution.py:248
  749.1 40.3 %reduce-scatter.15.cloned.1.call-done = bf16[192,1536]{1,0:T(8,128)(2,1)} async-done(((bf16[768,1536]{1,0:T(8,128)(2,1)}), bf16[192,1536]{1,0:T(8,128)(2,1)}) %reduce-scatter.15.cloned.1.call-update) | async-done | bytes 589840 | tf_op jit(solution)/shard_map/reduce_scatter | solution.py:245
  795.0 79.4 %all-reduce = (f32[2,384]{1,0:T(2,128)}, f32[1536]{0:T(1024)}, f32[2,768]{1,0:T(2,128)}, f32[4,768]{1,0:T(4,128)}) all-reduce(f32[2,384]{1,0:T(2,128)S(1)} %pad_maximum_fusion.5, f32[1536]{0:T(1024)} %get-tuple-element.353, f32[2,768]{1,0:T(2,128)S(1)} %pad_maximum_fusion.4, ...), channel_id=1, replica_groups=mesh['fsdp'=4,'context'=4,'tensor'=2] {'fsdp','context'}, use_global_device_ids=true, to_apply=%region_34.35 | all-reduce | flops 6912 | bytes 55296 | tf_op jit(solution)/shard_map/psum | solution.py:260
  877.0 21.2 %all-reduce.16.cloned.1.call-done = (bf16[3,192,384]{1,2,0:T(8,128)(2,1)}, bf16[384,192]{0,1:T(8,128)(2,1)}, bf16[192,1536]{1,0:T(8,128)(2,1)}, bf16[1536,192]{0,1:T(8,128)(2,1)}) async-done(((bf16[3,192,384]{1,2,0:T(8,128)(2,1)}, bf16[384,192]{0,1:T(8,128)(2,1)}, bf16[192,1536]{1,0:T(8,128)(2,1)}, bf16[1536,192]{0,1:T(8,128)(2,1)}), (bf16[3,192,384]{1,2,0:T(8,128)(2,1)}, bf16[384,192]{0,1:T(8,128)(2,1)}, ...) | async-done | bytes 1769488 | tf_op jit(solution)/shard_map/psum | solution.py:253
  (273 shorter events, 117.7 us)
Async XLA Ops:
  7.2 37.9 %all-gather.7.cloned.1.call-start = ((), (), s32[]{:S(2)}) async-start(), calls=%async_computation.6 | async-start | bytes 2211840 | tf_op jit(solution)/shard_map/all_gather | solution.py:78
  7.9 43.3 %copy-start.45 = (f32[2,384]{1,0:T(2,128)S(1)}, f32[2,384]{1,0:T(2,128)}, u32[]{:S(2)}) copy-start(f32[2,384]{1,0:T(2,128)} %param.19) | copy-start | bytes 9220
  7.9 93.3 %all-gather.15.cloned.1.call-start = ((), (), s32[]{:S(2)}) async-start(), calls=%async_computation.19 | async-start | bytes 2949120 | tf_op jit(solution)/shard_map/all_gather | solution.py:93
  50.2 3.4 copy-start.49
  50.2 4.3 copy-start.28
  50.2 15.9 %copy-start.43 = (s32[3072]{0:T(1024)S(1)}, s32[3072]{0:T(1024)}, u32[]{:S(2)}) copy-start(s32[3072]{0:T(1024)} %param.27) | copy-start | bytes 36868
  51.1 101.1 %all-gather.9.cloned.1.call-start = ((), (), s32[]{:S(2)}) async-start(), calls=%async_computation.7 | async-start | bytes 2949120 | tf_op jit(solution)/shard_map/all_gather | solution.py:94
  51.2 15.6 %slice-start = ((f32[3,768,384]{1,2,0:T(8,128)}), f32[1,768,384]{1,2,0:T(8,128)S(1)}, s32[]{:S(2)}) async-start(f32[3,768,384]{1,2,0:T(8,128)} %copy-done.13), calls=%async_computation.22 | async-start | bytes 2359296 | tf_op jit(solution)/shard_map/slice | solution.py:84
  53.6 219.4 %all-reduce.8.cloned.1.call-start = ((), (), s32[]{:S(2)}) async-start(), calls=%async_computation.8 | async-start | bytes 2359296 | tf_op jit(solution)/shard_map/psum | solution.py:130
  152.2 5.8 copy-start.14
  152.2 5.8 copy-start.22
  152.2 5.8 copy-start.25
  152.2 5.8 copy-start.29
  152.2 5.8 copy-start.36
  158.0 94.5 %copy-start.7 = (bf16[384,768]{0,1:T(8,128)(2,1)S(1)}, bf16[384,768]{0,1:T(8,128)(2,1)}, u32[]{:S(2)}) copy-start(bf16[384,768]{0,1:T(8,128)(2,1)} %all_gather.23) | copy-start | bytes 1769476
  250.7 147.1 %copy-start.23 = (f32[6,768]{1,0:T(8,128)}, f32[6,768]{1,0:T(8,128)S(1)}, u32[]{:S(2)}) copy-start(f32[6,768]{1,0:T(8,128)S(1)} %get-tuple-element.114) | copy-start | bytes 55300
  252.6 3.3 copy-start.44
  252.6 3.3 copy-start.42
  252.6 20.4 %copy-start = (bf16[768,768]{1,0:T(8,128)(2,1)S(1)}, bf16[768,768]{1,0:T(8,128)(2,1)}, u32[]{:S(2)}) copy-start(bf16[768,768]{1,0:T(8,128)(2,1)} %param.16) | copy-start | bytes 3538948
  254.4 58.8 %all-gather.11.cloned.1.call-start = ((), (), s32[]{:S(2)}) async-start(), calls=%async_computation.9 | async-start | bytes 2949120 | tf_op jit(solution)/shard_map/all_gather | solution.py:80
  255.0 97.3 %all-gather.13.cloned.1.call-start = ((), (), s32[]{:S(2)}) async-start(), calls=%async_computation.10 | async-start | bytes 2949120 | tf_op jit(solution)/shard_map/all_gather | solution.py:81
  255.6 122.0 %all-reduce.10.cloned.1.call-start = ((), (), s32[]{:S(2)}) async-start(), calls=%async_computation.11 | async-start | bytes 2359296 | tf_op jit(solution)/shard_map/psum | solution.py:141
  255.9 161.6 %copy-start.32 = (f32[768]{0:T(1024)}, f32[768]{0:T(1024)S(1)}, u32[]{:S(2)}) copy-start(f32[768]{0:T(1024)S(1)} %get-tuple-element.277) | copy-start | bytes 9220
  256.0 121.6 %copy-start.37 = (f32[768]{0:T(1024)}, f32[768]{0:T(1024)S(1)}, u32[]{:S(2)}) copy-start(f32[768]{0:T(1024)S(1)} %get-tuple-element.273) | copy-start | bytes 9220
  256.0 161.6 %copy-start.26 = (f32[768]{0:T(1024)}, f32[768]{0:T(1024)S(1)}, u32[]{:S(2)}) copy-start(f32[768]{0:T(1024)S(1)} %get-tuple-element.274) | copy-start | bytes 9220
  273.0 1.8 copy-start.1
  273.0 40.3 %copy-start.48 = (f32[1536]{0:T(1024)S(1)}, f32[1536]{0:T(1024)}, u32[]{:S(2)}) copy-start(f32[1536]{0:T(1024)} %param.22) | copy-start | bytes 18436
  274.9 142.7 %copy-start.30 = (f32[768]{0:T(1024)}, f32[768]{0:T(1024)S(1)}, u32[]{:S(2)}) copy-start(f32[768]{0:T(1024)S(1)} %broadcast_multiply_fusion.5) | copy-start | bytes 9220
  275.5 142.0 %copy-start.34 = (f32[768]{0:T(1024)}, f32[768]{0:T(1024)S(1)}, u32[]{:S(2)}) copy-start(f32[768]{0:T(1024)S(1)} %add_rsqrt_fusion.1) | copy-start | bytes 9220
  357.8 59.8 %all-reduce.12.cloned.1.call-start = ((), (), s32[]{:S(2)}) async-start(), calls=%async_computation.12 | async-start | bytes 2359296 | tf_op jit(solution)/shard_map/psum | solution.py:159
  382.9 1.9 copy-start.47
  384.8 7.3 copy-start.3
  384.8 8.6 copy-start.46
  396.5 189.5 %reduce-scatter.9.cloned.1.call-start = ((), (), s32[]{:S(2)}) async-start(), calls=%async_computation.13 | async-start | bytes 2949120 | tf_op jit(solution)/shard_map/reduce_scatter | solution.py:216
  417.6 4.0 copy-start.2
  417.6 4.0 copy-start.4
  417.6 4.0 copy-start.12
  421.5 2.8 copy-start.8
  435.2 3.3 copy-start.9
  441.2 2.9 copy-start.10
  452.9 3.3 copy-start.9
  458.9 2.9 copy-start.10
  470.6 3.3 copy-start.9
  476.6 2.9 copy-start.10
  488.3 3.3 copy-start.9
  494.3 2.9 copy-start.10
  506.0 3.3 copy-start.9
  512.0 2.9 copy-start.10
  523.7 3.3 copy-start.9
  529.7 2.9 copy-start.10
  537.0 98.3 %reduce-scatter.11.cloned.1.call-start = ((), (), s32[]{:S(2)}) async-start(), calls=%async_computation.14 | async-start | bytes 2949120 | tf_op jit(solution)/shard_map/reduce_scatter | solution.py:219
  541.3 138.6 %reduce-scatter.19.cloned.1.call-start = ((), (), s32[]{:S(2)}) async-start(), calls=%async_computation.20 | async-start | bytes 2211840
  647.9 60.8 %reduce-scatter.13.cloned.1.call-start = ((), (), s32[]{:S(2)}) async-start(), calls=%async_computation.16 | async-start | bytes 737280 | tf_op jit(solution)/shard_map/reduce_scatter | solution.py:242
  650.7 98.4 %reduce-scatter.17.cloned.1.call-start = ((), (), s32[]{:S(2)}) async-start(), calls=%async_computation.18 | async-start | bytes 2949120 | tf_op jit(solution)/shard_map/reduce_scatter | solution.py:248
  656.7 132.8 %reduce-scatter.15.cloned.1.call-start = ((), (), s32[]{:S(2)}) async-start(), calls=%async_computation.17 | async-start | bytes 2949120 | tf_op jit(solution)/shard_map/reduce_scatter | solution.py:245
  663.3 211.1 %all-reduce.14.cloned.1.call-start = ((), (), s32[]{:S(2)}) async-start(), calls=%async_computation.15 | async-start | bytes 2359296 | tf_op jit(solution)/shard_map/psum | solution.py:236
  669.0 123.0 %copy-start.40 = (f32[768]{0:T(1024)S(1)}, f32[768]{0:T(1024)}, u32[]{:S(2)}) copy-start(f32[768]{0:T(1024)} %get-tuple-element.263) | copy-start | bytes 9220
  669.0 123.6 %copy-start.39 = (f32[768]{0:T(1024)S(1)}, f32[768]{0:T(1024)}, u32[]{:S(2)}) copy-start(f32[768]{0:T(1024)} %get-tuple-element.268) | copy-start | bytes 9220
  669.0 123.6 %copy-start.38 = (f32[768]{0:T(1024)S(1)}, f32[768]{0:T(1024)}, u32[]{:S(2)}) copy-start(f32[768]{0:T(1024)} %get-tuple-element.269) | copy-start | bytes 9220
  669.0 123.6 %copy-start.41 = (f32[768]{0:T(1024)S(1)}, f32[768]{0:T(1024)}, u32[]{:S(2)}) copy-start(f32[768]{0:T(1024)} %get-tuple-element.338) | copy-start | bytes 9220
  669.0 124.2 %copy-start.11 = (bf16[6,768,64]{1,2,0:T(8,128)(2,1)S(1)}, bf16[6,768,64]{1,2,0:T(8,128)(2,1)}, u32[]{:S(2)}) copy-start(bf16[6,768,64]{1,2,0:T(8,128)(2,1)} %get-tuple-element.116) | copy-start | bytes 1769476
  669.0 229.1 %all-reduce.16.cloned.1.call-start = ((), (), s32[]{:S(2)}) async-start(), calls=%async_computation.21 | async-start | bytes 3833856 | tf_op jit(solution)/shard_map/psum | solution.py:253
  682.6 112.2 %copy-start.20 = (bf16[768,384]{1,0:T(8,128)(2,1)S(1)}, bf16[768,384]{1,0:T(8,128)(2,1)}, u32[]{:S(2)}) copy-start(bf16[768,384]{1,0:T(8,128)(2,1)} %reduce-scatter.11.cloned.1.call-done) | copy-start | bytes 1769476
  898.2 6.1 copy-start.18
  (14 other events, 15.3 us)
Sparse Core Ops, SparseCore 0:
  9.8 35.1 all-gather.6
  51.2 49.9 all-gather.14
  103.4 48.7 all-gather.8
  254.5 18.4 all-reduce.7
  274.7 38.5 all-gather.10
  315.0 37.3 all-gather.12
  357.9 19.6 all-reduce.9
  396.6 20.8 all-reduce.11
  537.1 48.8 reduce-scatter.8
  588.1 47.1 reduce-scatter.10
  648.0 31.8 reduce-scatter.18
  683.2 25.4 reduce-scatter.12
  711.7 37.3 reduce-scatter.16
  752.0 37.3 reduce-scatter.14
  792.2 19.6 all-reduce.13
  815.0 83.1 all-reduce.15
where the time goes:
time: 918 us; the launch traced here: 912 us
  waiting for transfers between devices  464 us (51%)
  matrix products  224 us (24%)
  blocking collectives  90.3 us (10%)
  other arithmetic  62 us (7%)
  local copies, waits for them, and re-layouts  56 us (6%)
  between operations  14.7 us (2%)
    psum x1, blocking collectives, shards(): lax.psum((grad_bias_qv, grad_bias_up, gain_rows, shift_rows), ('fsdp', 'c...  79.4 us
    reduce_scatter x1, waiting for transfers between devices, shards(): lax.psum_scatter(grad_values.astype(jnp.bfloat16), 'context', scatter_dim...  49.3 us
    all_gather x1, waiting for transfers between devices, shards(): value_piece = lax.all_gather(value_rows, 'context', axis=0, tiled=True)  45.2 us
    reduce_scatter x1, waiting for transfers between devices, shards(): lax.psum_scatter(grad_keys.astype(jnp.bfloat16), 'context', scatter_dimen...  42.3 us
    reduce_scatter x1, waiting for transfers between devices, shards(): lax.psum_scatter(grad_lower.astype(jnp.bfloat16), 'fsdp', scatter_dimensi...  40.4 us
    reduce_scatter x1, waiting for transfers between devices, shards(): lax.psum_scatter(grad_upper_w.astype(jnp.bfloat16), 'fsdp', scatter_dimen...  40.3 us
    all_gather x1, waiting for transfers between devices, shards(): lax.all_gather(w_up, 'fsdp', axis=0, tiled=True)  37.7 us
    all_gather x1, waiting for transfers between devices, shards(): lax.all_gather(w_qkv, 'fsdp', axis=1, tiled=True)  37.1 us
  transfers between devices with their start and end apart: 16, of which 15 were waited for; matrix products, arithmetic and copies ran while one was open for 8% of the time, Pallas kernels for 0%

commit v1 on v0

--- a/solution.py
+++ b/solution.py
@@ -61,6 +61,14 @@
     seq_lengths,
     key_mask,
 ):
+
+    def _measure_heads(content, s0, comm_axis):
+        return jnp.split(
+            lax.all_gather(jnp.concatenate([content, s0], axis=1), comm_axis, axis=0, tiled=True),
+            [content.shape[1]],
+            1,
+        )
+
     row_count = tokens.shape[0]
     local_width = w_qkv.shape[2]
     heads_here = local_width // 64
@@ -90,8 +98,7 @@
         jnp.zeros((heads_here, row_count), jnp.float32),
         jnp.zeros((heads_here, row_count, 64), jnp.float32),
     )
-    key_piece = lax.all_gather(key_rows, "context", axis=0, tiled=True)
-    value_piece = lax.all_gather(value_rows, "context", axis=0, tiled=True)
+    key_piece, value_piece = _measure_heads(key_rows, value_rows, "context")
     allowed = visible(key_piece.shape[0])
 
     def one_head(inputs):

time: 918 us -> 1020 us (1.11)
  waiting for transfers between devices: 464 us -> 529 us
  local copies, waits for them, and re-layouts: 56 us -> 89.3 us
    all_gather x0 -> x1, waiting for transfers between devices: none -> 71.5 us  [_measure_heads(): lax.all_gather(jnp.concatenate([content, s0], axis=1), comm_axis, axis=0,...]
    dynamic_update_slice x12, local copies, waits for them, and re-layouts: 1.03 us -> 16.3 us  [shards(): lax.map(one_head, (query_heads, split_heads(key_piece, heads_here), split...]
    reshape x2 -> x4, local copies, waits for them, and re-layouts: 11.5 us -> 21.3 us  [split_heads(): return matrix.reshape(matrix.shape[0], heads_here, 64).transpose(1, 0, 2)]
    unnamed x103 -> x97, local copies, waits for them, and re-layouts: 21.6 us -> 20.8 us
  transfers between devices with their start and end apart: 16 -> 17, of which waited for: 15 -> 16; matrix products, arithmetic and copies ran while one was open for 8% -> 9% of each run, Pallas kernels for 0% -> 0%
where the time goes in v1:
time: 1020 us; the launch traced here: 1010 us
  waiting for transfers between devices  529 us (52%)
  matrix products  223 us (22%)
  blocking collectives  90.3 us (9%)
  local copies, waits for them, and re-layouts  89.3 us (9%)
  other arithmetic  61.1 us (6%)
  between operations  14.8 us (1%)
    psum x1, blocking collectives, shards(): lax.psum((grad_bias_qv, grad_bias_up, gain_rows, shift_rows), ('fsdp', 'c...  79.4 us
    all_gather x1, waiting for transfers between devices, _measure_heads(): lax.all_gather(jnp.concatenate([content, s0], axis=1), comm_axis, axis=0,...  71.5 us
    reduce_scatter x1, waiting for transfers between devices, shards(): lax.psum_scatter(grad_values.astype(jnp.bfloat16), 'context', scatter_dim...  49.4 us
    all_gather x1, waiting for transfers between devices, shards(): value_piece = lax.all_gather(value_rows, 'context', axis=0, tiled=True)  44.5 us
    reduce_scatter x1, waiting for transfers between devices, shards(): lax.psum_scatter(grad_keys.astype(jnp.bfloat16), 'context', scatter_dimen...  42.5 us
    reduce_scatter x1, waiting for transfers between devices, shards(): lax.psum_scatter(grad_upper_w.astype(jnp.bfloat16), 'fsdp', scatter_dimen...  40.3 us
    reduce_scatter x1, waiting for transfers between devices, shards(): lax.psum_scatter(grad_lower.astype(jnp.bfloat16), 'fsdp', scatter_dimensi...  40.3 us
    all_gather x1, waiting for transfers between devices, shards(): lax.all_gather(w_up, 'fsdp', axis=0, tiled=True)  37.7 us
  transfers between devices with their start and end apart: 17, of which 16 were waited for; matrix products, arithmetic and copies ran while one was open for 9% of the time, Pallas kernels for 0%

profile of v1, /device:TPU:0, one launch (start us, length us, event | category | flops | bytes accessed | tf_op | source)
XLA Modules:
  0.0 1009.0 jit_solution(2827400862535599114)
XLA Ops:
  8.7 36.3 %all-gather.8.cloned.1.call-done = bf16[3,768,384]{2,1,0:T(8,128)(2,1)} async-done(((bf16[3,192,384]{2,1,0:T(8,128)(2,1)}), bf16[3,768,384]{2,1,0:T(8,128)(2,1)}) %all-gather.8.cloned.1.call-update) | async-done | bytes 1769488 | tf_op jit(solution)/shard_map/all_gather | solution.py:86
  45.1 3.4 convolution_bitcast_fusion
  52.0 10.9 %all_gather.23 = bf16[384,768]{0,1:T(8,128)(2,1)} all-gather(bf16[384,192]{0,1:T(8,128)(2,1)S(1)} %copy-done.28), channel_id=1, replica_groups=mesh['fsdp'=4,'context'=4,'tensor'=2] {'fsdp'}, dimensions={1}, use_global_device_ids=true | all-gather | bytes 737280 | tf_op jit(solution)/shard_map/all_gather | solution.py:87
  69.6 71.5 %all-gather.10.cloned.1.call-done = bf16[3072,768]{0,1:T(8,128)(2,1)} async-done(((bf16[768,768]{0,1:T(8,128)(2,1)}), bf16[3072,768]{0,1:T(8,128)(2,1)}) %all-gather.10.cloned.1.call-update) | async-done | bytes 4718608 | tf_op jit(solution)/shard_map/all_gather | solution.py:67
  141.2 4.1 fusion.102
  145.3 5.7 copy.57
  151.0 4.1 copy.58
  155.1 107.9 %while.32 = (s32[]{:T(128)}, f32[6,768]{1,0:T(8,128)}, f32[6,768]{1,0:T(8,128)}, f32[6,768,64]{1,2,0:T(8,128)S(1)}, bf16[6,768,64]{2,1,0:T(8,128)(2,1)}, /*index...) while((s32[]{:T(128)}, f32[6,768]{1,0:T(8,128)}, ...), condition=%wide.region_6.7_spmd.clone.clone, body=%wide.region_3.6_spmd.clone.sunk.clone | while | flops 658295808 | bytes 30426292 | solution.py:121
  155.1 5.0 select_reduce_fusion.3
  160.1 4.8 fusion.155
  164.9 5.4 fusion.156
  173.1 4.9 select_reduce_fusion.3
  178.0 4.8 fusion.155
  182.9 5.4 fusion.156
  191.0 4.9 select_reduce_fusion.3
  195.9 4.8 fusion.155
  200.8 5.4 fusion.156
  208.9 4.9 select_reduce_fusion.3
  213.8 4.8 fusion.155
  218.7 5.4 fusion.156
  226.8 4.9 select_reduce_fusion.3
  231.8 4.8 fusion.155
  236.6 5.4 fusion.156
  244.7 4.9 select_reduce_fusion.3
  249.7 4.8 fusion.155
  254.5 5.4 fusion.156
  268.0 16.9 %all-reduce.8.cloned.1.call-done = bf16[768,768]{1,0:T(8,128)(2,1)} async-done(((bf16[768,768]{1,0:T(8,128)(2,1)}), bf16[768,768]{1,0:T(8,128)(2,1)}) %all-reduce.8.cloned.1.call-update) | async-done | bytes 1179664 | tf_op jit(solution)/shard_map/psum | solution.py:137
  287.4 37.7 %all-gather.12.cloned.1.call-done = bf16[768,1536]{1,0:T(8,128)(2,1)} async-done(((bf16[192,1536]{1,0:T(8,128)(2,1)}), bf16[768,1536]{1,0:T(8,128)(2,1)}) %all-gather.12.cloned.1.call-update) | async-done | bytes 2359312 | tf_op jit(solution)/shard_map/all_gather | solution.py:88
  325.2 15.5 %multiply_convert_fusion.1 = (bf16[768,1536]{1,0:T(8,128)(2,1)}, f32[768,1536]{1,0:T(8,128)}, f32[768,1536]{1,0:T(8,128)}) fusion(f32[1536]{0:T(1024)S(1)} %copy-done.47, bf16[768,1536]{1,0:T(8,128)(2,1)} %all-gather.12.cloned.1.call-done, f32[768]{0:T(1024)S(1)} %get-tuple-element.273, f32[768]{0:T(1024)S(1)} %get-tuple-element.277, ...), kind=kOutput, calls=%fused_computation.67 | convolution fusion | flops 1895104512 | bytes 16536576 | tf_op jit(solution)/shard_map/dot_general | solution.py:143
  340.6 23.6 %all-gather.14.cloned.1.call-done = bf16[1536,768]{0,1:T(8,128)(2,1)} async-done(((bf16[1536,192]{0,1:T(8,128)(2,1)}), bf16[1536,768]{0,1:T(8,128)(2,1)}) %all-gather.14.cloned.1.call-update) | async-done | bytes 2359312 | tf_op jit(solution)/shard_map/all_gather | solution.py:89
  364.2 5.4 convolution_convert_fusion.4
  372.7 16.8 %all-reduce.10.cloned.1.call-done = bf16[768,768]{1,0:T(8,128)(2,1)} async-done(((bf16[768,768]{1,0:T(8,128)(2,1)}), bf16[768,768]{1,0:T(8,128)(2,1)}) %all-reduce.10.cloned.1.call-update) | async-done | bytes 1179664 | tf_op jit(solution)/shard_map/psum | solution.py:148
  396.7 7.5 convert_reduce_fusion
  409.6 32.6 %all-gather.18.cloned.1.call-done = bf16[1,3072,384]{1,2,0:T(8,128)(2,1)} async-done(((bf16[1,768,384]{1,2,0:T(8,128)(2,1)}), bf16[1,3072,384]{1,2,0:T(8,128)(2,1)}) %all-gather.18.cloned.1.call-update) | async-done | bytes 2359312 | tf_op jit(solution)/shard_map/all_gather | solution.py:184
  442.2 5.9 copy.59
  448.1 44.5 %all-gather.16.cloned.1.call-done = bf16[3072,384]{0,1:T(8,128)(2,1)} async-done(((bf16[768,384]{0,1:T(8,128)(2,1)}), bf16[3072,384]{0,1:T(8,128)(2,1)}) %all-gather.16.cloned.1.call-update) | async-done | bytes 2359312 | tf_op jit(solution)/shard_map/all_gather | solution.py:185
  492.6 5.7 copy.60
  498.9 15.0 %all-reduce.12.cloned.1.call-done = bf16[768,768]{1,0:T(8,128)(2,1)} async-done(((bf16[768,768]{1,0:T(8,128)(2,1)}), bf16[768,768]{1,0:T(8,128)(2,1)}) %all-reduce.12.cloned.1.call-update) | async-done | bytes 1179664 | tf_op jit(solution)/shard_map/psum | solution.py:166
  514.0 3.9 multiply_reduce_fusion
  522.9 106.1 %while.33 = (s32[]{:T(128)}, bf16[6,768,64]{1,2,0:T(8,128)(2,1)}, bf16[6,3072,64]{1,2,0:T(8,128)(2,1)}, bf16[6,3072,64]{1,2,0:T(8,128)(2,1)}, bf16[6,768,64]{2,1...) while((s32[]{:T(128)}, bf16[6,768,64]{1,2,0:T(8,128)(2,1)}, ...), condition=%wide.region_20.21_spmd.clone.clone, body=%wide.region_19.20_spmd.clone.sunk.clone | while | flops 1536147456 | bytes 51950792 | solution.py:208
  523.6 5.4 exponential_select_fusion.4
  531.6 3.3 multiply_convert_fusion.4
  541.3 5.4 exponential_select_fusion.4
  559.0 5.4 exponential_select_fusion.4
  567.0 3.3 multiply_convert_fusion.4
  576.7 5.4 exponential_select_fusion.4
  594.4 5.4 exponential_select_fusion.4
  612.1 5.4 exponential_select_fusion.4
  620.1 3.3 multiply_convert_fusion.4
  629.0 4.5 copy.62
  633.5 4.3 copy.63
  640.0 42.5 %reduce-scatter.9.cloned.1.call-done = bf16[768,384]{1,0:T(8,128)(2,1)} async-done(((bf16[3072,384]{1,0:T(8,128)(2,1)}), bf16[768,384]{1,0:T(8,128)(2,1)}) %reduce-scatter.9.cloned.1.call-update) | async-done | bytes 589840 | tf_op jit(solution)/shard_map/reduce_scatter | solution.py:223
  682.5 49.4 %reduce-scatter.11.cloned.1.call-done = bf16[768,384]{1,0:T(8,128)(2,1)} async-done(((bf16[3072,384]{1,0:T(8,128)(2,1)}), bf16[768,384]{1,0:T(8,128)(2,1)}) %reduce-scatter.11.cloned.1.call-update) | async-done | bytes 589840 | tf_op jit(solution)/shard_map/reduce_scatter | solution.py:226
  732.0 4.2 convert_bitcast_fusion
  736.2 5.2 copy.68
  747.4 5.8 convolution_convert_fusion
  754.0 5.9 convolution_convert_fusion.1
  761.1 4.4 bitcast_convert_fusion
  765.7 10.9 %reduce-scatter.19.cloned.1.call-done = bf16[192,1152]{1,0:T(8,128)(2,1)} async-done(((bf16[768,1152]{1,0:T(8,128)(2,1)}), bf16[192,1152]{1,0:T(8,128)(2,1)}) %reduce-scatter.19.cloned.1.call-update) | async-done | bytes 442384
  779.3 26.2 %reduce-scatter.13.cloned.1.call-done = bf16[384,192]{0,1:T(8,128)(2,1)} async-done(((bf16[384,768]{0,1:T(8,128)(2,1)}), bf16[384,192]{0,1:T(8,128)(2,1)}) %reduce-scatter.13.cloned.1.call-update) | async-done | bytes 147472 | tf_op jit(solution)/shard_map/reduce_scatter | solution.py:249
  805.5 40.3 %reduce-scatter.17.cloned.1.call-done = bf16[1536,192]{0,1:T(8,128)(2,1)} async-done(((bf16[1536,768]{0,1:T(8,128)(2,1)}), bf16[1536,192]{0,1:T(8,128)(2,1)}) %reduce-scatter.17.cloned.1.call-update) | async-done | bytes 589840 | tf_op jit(solution)/shard_map/reduce_scatter | solution.py:255
  845.8 40.3 %reduce-scatter.15.cloned.1.call-done = bf16[192,1536]{1,0:T(8,128)(2,1)} async-done(((bf16[768,1536]{1,0:T(8,128)(2,1)}), bf16[192,1536]{1,0:T(8,128)(2,1)}) %reduce-scatter.15.cloned.1.call-update) | async-done | bytes 589840 | tf_op jit(solution)/shard_map/reduce_scatter | solution.py:252
  891.7 79.4 %all-reduce = (f32[2,384]{1,0:T(2,128)}, f32[1536]{0:T(1024)}, f32[2,768]{1,0:T(2,128)}, f32[4,768]{1,0:T(4,128)}) all-reduce(f32[2,384]{1,0:T(2,128)S(1)} %pad_maximum_fusion.6, f32[1536]{0:T(1024)} %get-tuple-element.355, f32[2,768]{1,0:T(2,128)S(1)} %pad_maximum_fusion.5, ...), channel_id=1, replica_groups=mesh['fsdp'=4,'context'=4,'tensor'=2] {'fsdp','context'}, use_global_device_ids=true, to_apply=%region_34.35 | all-reduce | flops 6912 | bytes 55296 | tf_op jit(solution)/shard_map/psum | solution.py:267
  973.6 21.2 %all-reduce.16.cloned.1.call-done = (bf16[3,192,384]{1,2,0:T(8,128)(2,1)}, bf16[384,192]{0,1:T(8,128)(2,1)}, bf16[192,1536]{1,0:T(8,128)(2,1)}, bf16[1536,192]{0,1:T(8,128)(2,1)}) async-done(((bf16[3,192,384]{1,2,0:T(8,128)(2,1)}, bf16[384,192]{0,1:T(8,128)(2,1)}, bf16[192,1536]{1,0:T(8,128)(2,1)}, bf16[1536,192]{0,1:T(8,128)(2,1)}), (bf16[3,192,384]{1,2,0:T(8,128)(2,1)}, bf16[384,192]{0,1:T(8,128)(2,1)}, ...) | async-done | bytes 1769488 | tf_op jit(solution)/shard_map/psum | solution.py:260
  (298 shorter events, 148.9 us)
Async XLA Ops:
  7.2 37.9 %all-gather.8.cloned.1.call-start = ((), (), s32[]{:S(2)}) async-start(), calls=%async_computation.6 | async-start | bytes 2211840 | tf_op jit(solution)/shard_map/all_gather | solution.py:86
  7.9 133.2 %all-gather.10.cloned.1.call-start = ((), (), s32[]{:S(2)}) async-start(), calls=%async_computation.7 | async-start | bytes 5898240 | tf_op jit(solution)/shard_map/all_gather | solution.py:67
  50.4 16.2 %copy-start.12 = (bf16[768,384]{0,1:T(8,128)(2,1)}, bf16[768,384]{0,1:T(8,128)(2,1)S(1)}, u32[]{:S(2)}) copy-start(bf16[768,384]{0,1:T(8,128)(2,1)S(1)} %fusion.81) | copy-start | bytes 1769476
  50.4 13.2 %copy-start.43 = (s32[3072]{0:T(1024)S(1)}, s32[3072]{0:T(1024)}, u32[]{:S(2)}) copy-start(s32[3072]{0:T(1024)} %param.27) | copy-start | bytes 36868
  51.6 233.3 %all-reduce.8.cloned.1.call-start = ((), (), s32[]{:S(2)}) async-start(), calls=%async_computation.8 | async-start | bytes 2359296 | tf_op jit(solution)/shard_map/psum | solution.py:137
  151.0 4.1 copy-start.14
  155.1 109.7 %copy-start.7 = (bf16[384,768]{0,1:T(8,128)(2,1)S(1)}, bf16[384,768]{0,1:T(8,128)(2,1)}, u32[]{:S(2)}) copy-start(bf16[384,768]{0,1:T(8,128)(2,1)} %all_gather.23) | copy-start | bytes 1769476
  155.1 5.0 copy-start.25
  155.1 5.0 copy-start.29
  173.1 4.9 copy-start.25
  173.1 4.9 copy-start.29
  191.0 4.9 copy-start.25
  191.0 4.9 copy-start.29
  208.9 4.9 copy-start.25
  208.9 4.9 copy-start.29
  226.8 4.9 copy-start.25
  226.8 4.9 copy-start.29
  244.7 4.9 copy-start.25
  244.7 4.9 copy-start.29
  264.8 3.1 copy-start.44
  264.8 3.1 copy-start.42
  264.8 20.1 %copy-start = (bf16[768,768]{1,0:T(8,128)(2,1)S(1)}, bf16[768,768]{1,0:T(8,128)(2,1)}, u32[]{:S(2)}) copy-start(bf16[768,768]{1,0:T(8,128)(2,1)} %param.16) | copy-start | bytes 3538948
  266.7 58.5 %all-gather.12.cloned.1.call-start = ((), (), s32[]{:S(2)}) async-start(), calls=%async_computation.9 | async-start | bytes 2949120 | tf_op jit(solution)/shard_map/all_gather | solution.py:88
  267.2 97.0 %all-gather.14.cloned.1.call-start = ((), (), s32[]{:S(2)}) async-start(), calls=%async_computation.10 | async-start | bytes 2949120 | tf_op jit(solution)/shard_map/all_gather | solution.py:89
  267.8 121.6 %all-reduce.10.cloned.1.call-start = ((), (), s32[]{:S(2)}) async-start(), calls=%async_computation.11 | async-start | bytes 2359296 | tf_op jit(solution)/shard_map/psum | solution.py:148
  267.9 246.0 %copy-start.32 = (f32[768]{0:T(1024)}, f32[768]{0:T(1024)S(1)}, u32[]{:S(2)}) copy-start(f32[768]{0:T(1024)S(1)} %get-tuple-element.277) | copy-start | bytes 9220
  268.0 121.5 %copy-start.37 = (f32[768]{0:T(1024)}, f32[768]{0:T(1024)S(1)}, u32[]{:S(2)}) copy-start(f32[768]{0:T(1024)S(1)} %get-tuple-element.273) | copy-start | bytes 9220
  268.0 246.0 %copy-start.26 = (f32[768]{0:T(1024)}, f32[768]{0:T(1024)S(1)}, u32[]{:S(2)}) copy-start(f32[768]{0:T(1024)S(1)} %get-tuple-element.274) | copy-start | bytes 9220
  284.9 40.3 %copy-start.47 = (f32[1536]{0:T(1024)S(1)}, f32[1536]{0:T(1024)}, u32[]{:S(2)}) copy-start(f32[1536]{0:T(1024)} %param.22) | copy-start | bytes 18436
  286.7 227.2 %copy-start.30 = (f32[768]{0:T(1024)}, f32[768]{0:T(1024)S(1)}, u32[]{:S(2)}) copy-start(f32[768]{0:T(1024)S(1)} %broadcast_multiply_fusion.5) | copy-start | bytes 9220
  287.4 226.6 %copy-start.34 = (f32[768]{0:T(1024)}, f32[768]{0:T(1024)S(1)}, u32[]{:S(2)}) copy-start(f32[768]{0:T(1024)S(1)} %add_rsqrt_fusion.1) | copy-start | bytes 9220
  369.6 72.6 %all-gather.18.cloned.1.call-start = ((), (), s32[]{:S(2)}) async-start(), calls=%async_computation.20 | async-start | bytes 2949120 | tf_op jit(solution)/shard_map/all_gather | solution.py:184
  371.9 120.7 %all-gather.16.cloned.1.call-start = ((), (), s32[]{:S(2)}) async-start(), calls=%async_computation.13 | async-start | bytes 2949120 | tf_op jit(solution)/shard_map/all_gather | solution.py:185
  372.6 141.3 %all-reduce.12.cloned.1.call-start = ((), (), s32[]{:S(2)}) async-start(), calls=%async_computation.12 | async-start | bytes 2359296 | tf_op jit(solution)/shard_map/psum | solution.py:166
  396.7 7.5 copy-start.3
  396.7 8.9 copy-start.45
  408.7 273.8 %reduce-scatter.9.cloned.1.call-start = ((), (), s32[]{:S(2)}) async-start(), calls=%async_computation.14 | async-start | bytes 2949120 | tf_op jit(solution)/shard_map/reduce_scatter | solution.py:223
  492.6 5.7 copy-start.23
  492.6 5.7 copy-start.36
  514.0 4.0 copy-start.2
  514.0 4.0 copy-start.4
  514.0 4.0 copy-start.13
  531.6 3.3 copy-start.9
  537.6 2.9 copy-start.10
  549.3 3.3 copy-start.9
  555.3 2.9 copy-start.10
  567.0 3.3 copy-start.9
  584.7 3.3 copy-start.9
  602.4 3.3 copy-start.9
  620.1 3.3 copy-start.9
  633.5 98.5 %reduce-scatter.11.cloned.1.call-start = ((), (), s32[]{:S(2)}) async-start(), calls=%async_computation.15 | async-start | bytes 2949120 | tf_op jit(solution)/shard_map/reduce_scatter | solution.py:226
  637.8 138.8 %reduce-scatter.19.cloned.1.call-start = ((), (), s32[]{:S(2)}) async-start(), calls=%async_computation.21 | async-start | bytes 2211840
  744.6 60.9 %reduce-scatter.13.cloned.1.call-start = ((), (), s32[]{:S(2)}) async-start(), calls=%async_computation.17 | async-start | bytes 737280 | tf_op jit(solution)/shard_map/reduce_scatter | solution.py:249
  747.4 98.4 %reduce-scatter.17.cloned.1.call-start = ((), (), s32[]{:S(2)}) async-start(), calls=%async_computation.19 | async-start | bytes 2949120 | tf_op jit(solution)/shard_map/reduce_scatter | solution.py:255
  753.3 132.8 %reduce-scatter.15.cloned.1.call-start = ((), (), s32[]{:S(2)}) async-start(), calls=%async_computation.18 | async-start | bytes 2949120 | tf_op jit(solution)/shard_map/reduce_scatter | solution.py:252
  759.9 211.2 %all-reduce.14.cloned.1.call-start = ((), (), s32[]{:S(2)}) async-start(), calls=%async_computation.16 | async-start | bytes 2359296 | tf_op jit(solution)/shard_map/psum | solution.py:243
  765.6 123.1 %copy-start.40 = (f32[768]{0:T(1024)S(1)}, f32[768]{0:T(1024)}, u32[]{:S(2)}) copy-start(f32[768]{0:T(1024)} %get-tuple-element.263) | copy-start | bytes 9220
  765.6 123.7 %copy-start.39 = (f32[768]{0:T(1024)S(1)}, f32[768]{0:T(1024)}, u32[]{:S(2)}) copy-start(f32[768]{0:T(1024)} %get-tuple-element.268) | copy-start | bytes 9220
  765.6 123.7 %copy-start.38 = (f32[768]{0:T(1024)S(1)}, f32[768]{0:T(1024)}, u32[]{:S(2)}) copy-start(f32[768]{0:T(1024)} %get-tuple-element.269) | copy-start | bytes 9220
  765.6 123.7 %copy-start.41 = (f32[768]{0:T(1024)S(1)}, f32[768]{0:T(1024)}, u32[]{:S(2)}) copy-start(f32[768]{0:T(1024)} %get-tuple-element.338) | copy-start | bytes 9220
  765.6 124.3 %copy-start.11 = (bf16[6,768,64]{1,2,0:T(8,128)(2,1)S(1)}, bf16[6,768,64]{1,2,0:T(8,128)(2,1)}, u32[]{:S(2)}) copy-start(bf16[6,768,64]{1,2,0:T(8,128)(2,1)} %get-tuple-element.116) | copy-start | bytes 1769476
  765.6 229.2 %all-reduce.16.cloned.1.call-start = ((), (), s32[]{:S(2)}) async-start(), calls=%async_computation.22 | async-start | bytes 3833856 | tf_op jit(solution)/shard_map/psum | solution.py:260
  779.3 112.2 %copy-start.21 = (bf16[768,384]{1,0:T(8,128)(2,1)S(1)}, bf16[768,384]{1,0:T(8,128)(2,1)}, u32[]{:S(2)}) copy-start(bf16[768,384]{1,0:T(8,128)(2,1)} %reduce-scatter.11.cloned.1.call-done) | copy-start | bytes 1769476
  994.8 6.1 copy-start.19
  (23 other events, 36.6 us)
Sparse Core Ops, SparseCore 0:
  9.8 35.1 all-gather.7
  51.7 89.3 all-gather.9
  266.8 18.0 all-reduce.7
  286.6 38.5 all-gather.11
  326.8 37.3 all-gather.13
  369.8 19.6 all-reduce.9
  391.0 51.1 all-gather.17
  443.8 48.7 all-gather.15
  495.5 18.4 all-reduce.11
  633.6 48.8 reduce-scatter.8
  684.8 47.0 reduce-scatter.10
  744.7 31.8 reduce-scatter.18
  780.0 25.4 reduce-scatter.12
  808.4 37.3 reduce-scatter.16
  848.7 37.3 reduce-scatter.14
  888.9 19.6 all-reduce.13
  911.6 83.1 all-reduce.15
